TPU v7x, 32 devices: a whole 2x2x4 slice. The times are simulated.
32 devices in a mesh: group: 2 (over y), lon: 16 (over z, x, core).
Axes of the slice: x: 2, y: 2, z: 4, core: 2. Of those that a mesh axis runs over, the one named last changes fastest.
Arguments:
- tokens: bfloat16 [128, 32, 64, 128], P('group', 'lon'), parts along dimension 0, may hold values from -600 to 600, as said below
- neighbours: int32 [64, 32, 9], P(None, 'lon'), may hold values from 0 to 2047, as said below
- time_step: int32 [2], P('group'), parts along dimension 0, may hold values from 0 to 999
- time_weight: bfloat16 [256, 128], replicated, may hold values from -0.375 to 0.375
- fine_project: bfloat16 [128, 384], replicated, may hold values from -0.5 to 0.5
- fine_output: bfloat16 [128, 128], replicated, may hold values from -0.5 to 0.5
- fine_scale: float32 [2], replicated, may hold values from 8 to 400
- coarse_input: bfloat16 [128, 1024], replicated, may hold values from -0.5 to 0.5
- coarse_project: bfloat16 [1024, 3072], replicated, may hold values from -0.1875 to 0.1875
- coarse_scale: float32 [16], replicated, may hold values from 8 to 400
- coarse_output: bfloat16 [1024, 128], replicated, may hold values from -0.1875 to 0.1875
Outputs:
- update: bfloat16 [128, 32, 64, 128], P('group', 'lon'), parts along dimension 0
There are 2 independent parts, one for each index of `group`. A program takes and returns all parts, laid end to end along the dimension named above; an argument that names none is the same for every part. Nothing has to cross between parts.
Inputs may be any that keep to these rules, and one draw needn't show every extreme that they name: `tokens`: values carry scales that differ from token to token and from feature to feature. `neighbours`: entry s of a tile's list names a tile whose longitude column is the tile's plus s // 3 - 1, cyclically over 32 columns, and whose latitude row lies within one of the tile's, clamped to 0 .. 63; entry 4 is the tile itself.
All inputs are finite; a program needn't handle non-finite values.
Results may differ from a plain program's by a relative error of at most 0.025.
Values may be sent and summed in bfloat16 or wider, within the bound.
No kernel may reach another device: no remote copies, remote signals or barrier semaphores. Data moves between devices by JAX's collectives and lax.ppermute only.
A program may use at most 128 MiB of HBM per device.

v0:
```python
import math

import jax
import jax.numpy as jnp
from jax import lax
from jax.sharding import PartitionSpec as P

HD = 64
TILE = 8
POOL = 32


EPS = 1e-06


def with_halo(value, sides, width):
    for axis, dim in sides:
        size, length = (lax.axis_size(axis), value.shape[dim])
        up = [(i, (i + 1) % size) for i in range(size)]
        down = [(j, i) for i, j in up]
        last = lax.slice_in_dim(value, length - width, length, axis=dim)
        first = lax.slice_in_dim(value, 0, width, axis=dim)
        before = lax.ppermute(last, axis, up)
        after = lax.ppermute(first, axis, down)
        value = jnp.concatenate([before, value, after], axis=dim)
    return value


def partner(value, axis, stride):
    mask = 2**stride
    pairs = [(source, source ^ mask) for source in range(lax.axis_size(axis))]
    return lax.ppermute(value, axis, pairs)


def time_features(time_step, size):
    half = size // 2
    freqs = jnp.exp(jnp.arange(half, dtype=jnp.float32) * (-math.log(10000.0) / half))
    angles = time_step.astype(jnp.float32)[0] * freqs
    return jnp.concatenate([jnp.cos(angles), jnp.sin(angles)])


def head_normal(values, head_size):
    shaped = values.reshape(values.shape[:-1] + (values.shape[-1] // head_size, head_size))
    scaled = shaped * lax.rsqrt(jnp.sum(shaped * shaped, axis=-1, keepdims=True) + EPS)
    return scaled.reshape(values.shape)


def pair_rows(projected, width, head_size):
    keys = head_normal(projected[:, :width], head_size).astype(jnp.bfloat16)
    values = projected[:, width:].astype(jnp.bfloat16)
    return (keys, values)


def local_attend(query, keys, values, head_size):
    count, rows, width = query.shape
    heads = width // head_size
    length = keys.shape[1]
    query_heads = query.reshape(count, rows, heads, head_size)
    key_heads = keys.reshape(count, length, heads, head_size)
    value_heads = values.reshape(count, length, heads, head_size)
    scores = jnp.einsum(
        "tqhd,tkhd->thqk", query_heads, key_heads, preferred_element_type=jnp.float32
    )
    largest = jnp.max(scores, axis=-1, keepdims=True)
    raised = jnp.exp(scores - largest)
    totals = jnp.sum(raised, axis=-1)
    mixed = jnp.einsum(
        "thqk,tkhd->tqhd",
        raised.astype(jnp.bfloat16),
        value_heads,
        preferred_element_type=jnp.float32,
    )
    mixed = mixed / jnp.transpose(totals, (0, 2, 1))[..., None]
    return mixed.reshape(count, rows, width).astype(jnp.bfloat16)


def absorb(carry, query, keys, values, head_size):
    maxima, totals, weighted = carry
    rows, width = query.shape
    heads = width // head_size
    query_heads = query.reshape(rows, heads, head_size)
    key_heads = keys.reshape(keys.shape[0], heads, head_size)
    value_heads = values.reshape(values.shape[0], heads, head_size)
    scores = jnp.einsum("qhd,khd->hqk", query_heads, key_heads, preferred_element_type=jnp.float32)
    newest = jnp.maximum(maxima, jnp.max(scores, axis=-1))
    raised = jnp.exp(scores - newest[..., None])
    totals = jnp.sum(raised, axis=-1)
    added = jnp.einsum(
        "hqk,khd->qhd", raised.astype(jnp.bfloat16), value_heads, preferred_element_type=jnp.float32
    )
    weighted = added
    return (newest, totals, weighted)


def shards(
    tokens,
    neighbours,
    time_step,
    time_weight,
    fine_project,
    fine_output,
    fine_scale,
    coarse_input,
    coarse_project,
    coarse_scale,
    coarse_output,
):
    lat_tiles, columns, cells, width = tokens.shape
    global_width = coarse_input.shape[1]
    features = time_features(time_step, time_weight.shape[0])
    modulation = jnp.dot(
        features.astype(jnp.bfloat16)[None, :], time_weight, preferred_element_type=jnp.float32
    )[0]
    values32 = tokens.astype(jnp.float32)
    factor = lax.rsqrt(jnp.mean(values32 * values32, axis=-1, keepdims=True) + EPS)
    normed = (values32 * factor * (1.0 + modulation)).astype(jnp.bfloat16)
    projected = jnp.dot(normed.reshape(-1, width), fine_project, preferred_element_type=jnp.float32)
    query = (head_normal(projected[:, :width], HD) * jnp.repeat(fine_scale, HD)).astype(
        jnp.bfloat16
    )
    own_keys, own_values = pair_rows(projected[:, width:], width, HD)
    own_pairs = jnp.concatenate([own_keys, own_values], axis=-1).reshape(
        lat_tiles, columns, cells, 2 * width
    )
    padded = with_halo(own_pairs, (("lon", 1),), 1)
    total_columns = columns * lax.axis_size("lon")
    row_iota = jnp.arange(lat_tiles, dtype=jnp.int32)[:, None, None]
    row_step = neighbours // total_columns - row_iota
    extended = jnp.concatenate([padded[:1], padded, padded[-1:]], axis=0)
    blocks = lat_tiles // 4
    query_blocks = query.reshape(blocks, 4 * columns, cells, width)
    step_blocks = row_step.reshape(blocks, 4, columns, 9)
    block_ids = jnp.arange(blocks, dtype=jnp.int32)

    def attend_block(block_args):
        query_block, step_block, block_id = block_args
        window = lax.dynamic_slice_in_dim(extended, block_id * 4, 6, 0)
        pieces = []
        for slot in range(9):
            offset = slot // 3
            strip = window[:, offset : offset + columns]
            step = step_block[:, :, slot][:, :, None, None]
            pieces.append(
                jnp.where(step < 0, strip[0:4], jnp.where(step > 0, strip[2:6], strip[1:5]))
            )
        gathered = jnp.concatenate(pieces, axis=2).reshape(4 * columns, 9 * cells, 2 * width)
        return local_attend(query_block, gathered[..., :width], gathered[..., width:], HD)

    fine_mixed = lax.map(attend_block, (query_blocks, step_blocks, block_ids))
    fine_update = jnp.dot(
        fine_mixed.reshape(-1, width), fine_output, preferred_element_type=jnp.float32
    )
    side = POOL // TILE
    cell_rows = lat_tiles // side
    partial_value = jnp.sum(
        normed.reshape(cell_rows, side, columns, cells, width), axis=(1, 2, 3), dtype=jnp.float32
    )
    pair_size = POOL // (TILE * columns)
    partial_value = partial_value + partner(partial_value, "lon", 0)
    pooled = (partial_value / (POOL * POOL)).astype(jnp.bfloat16)
    raw = jnp.dot(pooled, coarse_input, preferred_element_type=jnp.float32)
    coarse = (raw * lax.rsqrt(jnp.mean(raw * raw, axis=-1, keepdims=True) + EPS)).astype(
        jnp.bfloat16
    )
    own_count = cell_rows // pair_size
    half_index = lax.axis_index("lon") % pair_size
    heads = global_width // HD
    sub_width = global_width // pair_size
    sub_heads = heads // pair_size
    col_start = half_index * sub_width
    query_weight = lax.dynamic_slice_in_dim(coarse_project, col_start, sub_width, 1)
    scale_share = lax.dynamic_slice_in_dim(coarse_scale, half_index * sub_heads, sub_heads, 0)
    coarse_query = jnp.dot(coarse, query_weight, preferred_element_type=jnp.float32)
    coarse_query = (head_normal(coarse_query, HD) * jnp.repeat(scale_share, HD)).astype(
        jnp.bfloat16
    )
    own_cells = lax.dynamic_slice_in_dim(coarse, half_index * own_count, own_count, 0)
    start_carry = (
        jnp.full((sub_heads, cell_rows), -1e30, jnp.float32),
        jnp.zeros((sub_heads, cell_rows), jnp.float32),
        jnp.zeros((cell_rows, sub_heads, HD), jnp.float32),
    )
    pair_weight = coarse_project[:, global_width:]
    cell_keys, cell_values = pair_rows(
        jnp.dot(own_cells, pair_weight, preferred_element_type=jnp.float32), global_width, HD
    )
    piece_keys = lax.dynamic_slice_in_dim(
        lax.all_gather(cell_keys, "lon", axis=0, tiled=True), col_start, sub_width, 1
    )
    piece_values = lax.dynamic_slice_in_dim(
        lax.all_gather(cell_values, "lon", axis=0, tiled=True), col_start, sub_width, 1
    )
    maxima, totals, weighted = absorb(start_carry, coarse_query, piece_keys, piece_values, HD)
    coarse_mixed = (
        (weighted / jnp.transpose(totals)[..., None])
        .reshape(cell_rows, sub_width)
        .astype(jnp.bfloat16)
    )
    output_rows = lax.dynamic_slice_in_dim(coarse_output, col_start, sub_width, 0)
    coarse_update = jnp.dot(coarse_mixed, output_rows, preferred_element_type=jnp.float32)
    coarse_update = coarse_update + partner(coarse_update, "lon", 0)
    update = (
        fine_update.reshape(cell_rows, side, columns, cells, width)
        + coarse_update[:, None, None, None, :]
    )
    return update.reshape(lat_tiles, columns, cells, width).astype(jnp.bfloat16)


def solution(mesh):
    return jax.shard_map(
        shards,
        mesh=mesh,
        in_specs=(
            P("group", "lon", None, None),
            P(None, "lon", None),
            P("group"),
            P(),
            P(),
            P(),
            P(),
            P(),
            P(),
            P(),
            P(),
        ),
        out_specs=P("group", "lon", None, None),
        check_vma=False,
    )
```

profile of v0, /device:TPU:0, one launch (start us, length us, event | category | flops | bytes accessed | tf_op | source)
XLA Modules:
  0.0 645.1 jit_solution(7392557143895449796)
XLA Ops:
  11.2 3.6 copy-done.3
  16.6 4.5 fusion.33
  23.3 6.4 copy.41
  29.7 4.9 fusion.66
  34.6 5.6 collective-permute-start.1
  46.1 51.1 %all_gather.7 = bf16[128,1024]{1,0:T(8,128)(2,1)S(1)} all-gather(bf16[8,1024]{1,0:T(8,128)(2,1)S(1)} %multiply_convert_fusion.1), channel_id=1, replica_groups=mesh['group'=2,'lon'=16] {'lon'}, dimensions={0}, use_global_device_ids=true | all-gather | bytes 278528 | tf_op jit(solution)/shard_map/all_gather | solution.py:188
  97.3 20.4 %all_gather.6 = bf16[128,1024]{1,0:T(8,128)(2,1)S(1)} all-gather(bf16[8,1024]{1,0:T(8,128)(2,1)S(1)} %slice.192), channel_id=1, replica_groups=mesh['group'=2,'lon'=16] {'lon'}, dimensions={0}, use_global_device_ids=true | all-gather | bytes 278528 | tf_op jit(solution)/shard_map/all_gather | solution.py:191
  121.7 16.5 %fusion.26 = bf16[66,4,64,256]{3,2,1,0:T(8,128)(2,1)} fusion(bf16[64,1,64,256]{3,2,1,0:T(8,128)(2,1)} %collective-permute-done.1, bf16[64,2,64,256]{3,2,1,0:T(8,128)(2,1)} %bitcast.100, bf16[64,1,64,256]{3,2,1,0:T(8,128)(2,1)} %collective-permute-done), kind=kLoop, calls=%fused_computation.60 | loop fusion | flops 112459776 | bytes 17039360 | tf_op jit(solution)/shard_map/concatenate | solution.py:129
  138.2 502.1 %while.10 = (s32[]{:T(128)}, bf16[16,8,64,128]{2,3,1,0:T(8,128)(2,1)}, s32[16,4,2,9]{3,2,1,0:T(2,128)S(1)}, s32[16]{0:T(128)S(1)}, bf16[66,4,64,256]{3,2,1,0:T(8...) while((s32[]{:T(128)}, ...), condition=%wide.region_6.7_spmd, body=%wide.region_3.6_spmd.sunk | while | flops 231344416 | bytes 42608560 | solution.py:149
  153.2 5.2 concatenate.23
  184.6 5.2 concatenate.23
  216.0 5.2 concatenate.23
  224.2 3.3 fusion.103
  247.3 5.2 concatenate.23
  255.5 3.3 fusion.103
  278.7 5.2 concatenate.23
  310.2 5.2 concatenate.23
  341.5 5.2 concatenate.23
  349.7 3.3 fusion.103
  372.8 5.2 concatenate.23
  404.1 5.2 concatenate.23
  412.3 3.3 fusion.103
  435.5 5.2 concatenate.23
  466.9 5.2 concatenate.23
  498.3 5.2 concatenate.23
  506.5 3.3 fusion.103
  529.6 5.2 concatenate.23
  561.0 5.2 concatenate.23
  592.3 5.2 concatenate.23
  609.8 3.3 constant_dynamic-slice_fusion.14
  624.0 5.2 concatenate.23
  640.3 4.8 add_convert_fusion
  (492 shorter events, 411.5 us)
Async XLA Ops:
  0.0 40.5 %copy-start = (bf16[128,1024]{1,0:T(8,128)(2,1)S(1)}, bf16[128,1024]{1,0:T(8,128)(2,1)}, u32[]{:S(2)}) copy-start(bf16[128,1024]{1,0:T(8,128)(2,1)} %param.20) | copy-start | bytes 786436
  0.0 8.4 %copy-start.6 = (bf16[128,384]{1,0:T(8,128)(2,1)S(1)}, bf16[128,384]{1,0:T(8,128)(2,1)}, u32[]{:S(2)}) copy-start(bf16[128,384]{1,0:T(8,128)(2,1)} %param.17) | copy-start | bytes 294916
  7.8 32.6 %collective-permute-start.2 = (f32[16,128]{1,0:T(8,128)S(1)}, f32[16,128]{1,0:T(8,128)S(1)}, u32[]{:S(2)}, u32[]{:S(2)}) collective-permute-start(f32[16,128]{1,0:T(8,128)S(1)} %reduce_sum.93), channel_id=1, source_target_pairs={{0,1},{1,0},{2,3},{3,2},{4,5},{5,4},{6,7},{7,6},{8,9},{9,8},{10,11... | collective-permute-start | bytes 24584 | tf_op jit(solution)/shard_map/ppermute | solution.py:32
  10.2 4.6 copy-start.3
  16.6 4.5 copy-start.5
  29.7 10.5 %copy-start.11 = (f32[16]{0:T(128)S(1)}, f32[16]{0:T(128)}, u32[]{:S(2)}) copy-start(f32[16]{0:T(128)} %param.22) | copy-start | bytes 196
  34.6 87.1 %collective-permute-start = (bf16[64,1,64,256]{3,2,1,0:T(8,128)(2,1)}, bf16[64,1,64,256]{3,2,1,0:T(8,128)(2,1)}, u32[]{:S(2)}, u32[]{:S(2)}) collective-permute-start(bf16[64,1,64,256]{3,2,1,0:T(8,128)(2,1)} %get-tuple-element.121), channel_id=1, source_target_pairs={{0,1},{1,2},{2,3},{3,4},{4,5},{5,6},{6,7},{7,8},{8,9},{9,10},{10,1... | collective-permute-start | bytes 6291464 | tf_op jit(solution)/shard_map/ppermute | solution.py:23
  34.6 87.1 %collective-permute-start.1 = (bf16[64,1,64,256]{3,2,1,0:T(8,128)(2,1)}, bf16[64,1,64,256]{3,2,1,0:T(8,128)(2,1)}, u32[]{:S(2)}, u32[]{:S(2)}) collective-permute-start(bf16[64,1,64,256]{3,2,1,0:T(8,128)(2,1)} %get-tuple-element.122), channel_id=1, source_target_pairs={{1,0},{2,1},{3,2},{4,3},{5,4},{6,5},{7,6},{8,7},{9,8},{10,9},{11,1... | collective-permute-start | bytes 6291464 | tf_op jit(solution)/shard_map/ppermute | solution.py:24
  40.8 77.8 %copy-start.7 = (bf16[1024,128]{1,0:T(8,128)(2,1)S(1)}, bf16[1024,128]{1,0:T(8,128)(2,1)}, u32[]{:S(2)}) copy-start(bf16[1024,128]{1,0:T(8,128)(2,1)} %param.23) | copy-start | bytes 786436
  40.8 78.3 %copy-start.9 = (s32[64,2,9]{0,1,2:T(2,128)S(1)}, s32[64,2,9]{0,1,2:T(2,128)}, u32[]{:S(2)}) copy-start(s32[64,2,9]{0,1,2:T(2,128)} %param.14) | copy-start | bytes 13828
  118.7 3.0 collective-permute-start.3
  138.2 502.1 %copy-start.8 = (bf16[128,128]{1,0:T(8,128)(2,1)S(1)}, bf16[128,128]{1,0:T(8,128)(2,1)}, u32[]{:S(2)}) copy-start(bf16[128,128]{1,0:T(8,128)(2,1)} %param.18) | copy-start | bytes 98308
  160.2 5.3 copy-start.4
  191.6 5.3 copy-start.4
  223.0 4.5 copy-start.2
  223.0 5.3 copy-start.4
  254.3 5.3 copy-start.4
  285.7 5.3 copy-start.4
  317.2 5.3 copy-start.4
  348.5 5.3 copy-start.4
  379.8 5.3 copy-start.4
  411.1 4.5 copy-start.2
  411.1 5.3 copy-start.4
  442.5 5.3 copy-start.4
  473.9 5.3 copy-start.4
  505.3 4.5 copy-start.2
  505.3 5.3 copy-start.4
  536.6 5.3 copy-start.4
  568.0 5.3 copy-start.4
  599.3 5.3 copy-start.4
  631.0 5.3 copy-start.4
  640.3 4.8 copy-start.1
  (14 other events, 59.9 us)
where the time goes:
time: 653 us; the launch traced here: 645 us
  local copies, waits for them, and re-layouts  301 us (46%)
  matrix products  130 us (20%)
  other arithmetic  123 us (19%)
  blocking collectives  71.4 us (11%)
  loops' own time  11.9 us (2%)
  starting transfers between devices  6.53 us (1%)
    concatenate x16, local copies, waits for them, and re-layouts, attend_block(): jnp.concatenate(pieces, axis=2).reshape(4 * columns, 9 * cells, 2 * width)  83.3 us
    while x208, local copies, waits for them, and re-layouts  82.1 us
    select_n x32, other arithmetic, attend_block(): jnp.where(step < 0, strip[0:4], jnp.where(step > 0, strip[2:6], strip[1:5]))  70.1 us
    dot_general x16, matrix products, local_attend(): jnp.einsum('tqhd,tkhd->thqk', query_heads, key_heads, preferred_element_t...  52.3 us
    dot_general x16, matrix products, local_attend(): jnp.einsum('thqk,tkhd->tqhd', raised.astype(jnp.bfloat16), value_heads, p...  52 us
    all_gather x1, blocking collectives, shards(): lax.all_gather(cell_keys, 'lon', axis=0, tiled=True)  51.1 us
    slice x16, local copies, waits for them, and re-layouts, attend_block(): strip[1:5]  46.8 us
    slice x16, local copies, waits for them, and re-layouts, attend_block(): gathered[..., :width]  28.2 us
  transfers between devices with their start and end apart: 4, of which 0 were waited for; matrix products, arithmetic and copies ran while one was open for 5% of the time, Pallas kernels for 0%

commit v1 on v0

v1 whole, which is shorter than its diff:
```python
import math, functools
import numpy as np
import jax, jax.numpy as jnp
from jax import lax
from jax.sharding import PartitionSpec as P
from jax.experimental import pallas as pl
from jax.experimental.pallas import tpu as pltpu

EPS = 1e-6
LOG2E = math.log2(math.e)
HD = 64
TILE = 8
POOL = 32
bf16, f32 = jnp.bfloat16, jnp.float32
NT = (((1,), (1,)), ((), ()))
NN = (((1,), (0,)), ((), ()))

def dot(a, b, dims=NN):
    return lax.dot_general(a, b, dims, preferred_element_type=f32)

def block_sum(values, ones):
    high = values.astype(bf16)
    low = (values - high.astype(f32)).astype(bf16)
    return dot(jnp.concatenate([high, low], axis=1), ones)

def normed_of(x, gain, ones):
    v = x.astype(f32)
    mean = jnp.mean(v * v, axis=-1, keepdims=True)
    return (v * lax.rsqrt(mean + EPS) * gain).astype(bf16)

def ones_block(width, size):
    blocks = np.kron(np.eye(width // size), np.ones((size, size)))
    return np.concatenate([blocks, blocks], axis=0)

def project_kernel(with_query, rows, tok_ref, gain_ref, wqk_ref, wvt_ref, ones_ref, scale_ref, *outs):
    i = pl.program_id(1)
    if with_query:
        q_ref, k_ref, vt_ref = outs
    else:
        k_ref, vt_ref = outs
    cells = tok_ref.shape[-2]
    width = tok_ref.shape[-1]
    n = rows * cells
    x = tok_ref[...].reshape(n, width)
    normed = normed_of(x, gain_ref[...], None)
    ones = ones_ref[...]
    qk = dot(normed, wqk_ref[...])
    if with_query:
        q = qk[:, :width]
        q = q * lax.rsqrt(block_sum(q * q, ones) + EPS) * scale_ref[...]
        q_ref[0] = q.astype(bf16)
        k = qk[:, width:]
    else:
        k = qk
    k = k * lax.rsqrt(block_sum(k * k, ones) + EPS)
    k_ref[0] = k.astype(bf16)
    vt_ref[0] = dot(wvt_ref[...], normed, NT).astype(bf16)

def project(tokens, gain, wqk, wvt, ones, scale, with_query, rows=8):
    lat, columns, cells, width = tokens.shape
    n = rows * cells
    const = lambda a: pl.BlockSpec(a.shape, lambda c, i: (0,) * a.ndim)
    tshape = jax.ShapeDtypeStruct((columns, lat * cells, width), bf16)
    vshape = jax.ShapeDtypeStruct((columns, width, lat * cells), bf16)
    tspec = pl.BlockSpec((1, n, width), lambda c, i: (c, i, 0))
    vspec = pl.BlockSpec((1, width, n), lambda c, i: (c, 0, i))
    outs = [tshape, vshape]; specs = [tspec, vspec]
    if with_query:
        outs = [tshape] + outs; specs = [tspec] + specs
    return pl.pallas_call(
        functools.partial(project_kernel, with_query, rows),
        grid=(columns, lat // rows),
        in_specs=[pl.BlockSpec((rows, 1, cells, width), lambda c, i: (i, c, 0, 0)),
                  const(gain), const(wqk), const(wvt), const(ones), const(scale)],
        out_specs=specs, out_shape=outs, name="project",
    )(tokens, gain, wqk, wvt, ones, scale)

def attend_kernel(rows, ncol, lw_ref, *refs):
    q_refs = refs[:ncol]
    k_refs = refs[ncol:2 * ncol + 2]
    v_refs = refs[2 * ncol + 2:3 * ncol + 4]
    wo_ref, cu_ref, out_ref, p_ref = refs[3 * ncol + 4:]
    i = pl.program_id(0)
    cells = HD
    width = wo_ref.shape[0]

    @pl.when(i == 0)
    def _():
        p_ref[...] = jnp.zeros_like(p_ref)

    lane = lax.broadcasted_iota(jnp.int32, (cells, width), 1)
    first = lane < HD
    wo = wo_ref[...]

    def pair_rows(p, carry):
        off = pl.multiple_of(p * 2 * cells, 2 * cells)
        for c in range(ncol):
            q2 = q_refs[c][0, pl.ds(off, 2 * cells), :]
            zero = jnp.zeros((cells, width), bf16)
            qbd = jnp.concatenate(
                [jnp.where(first, q2[:cells], zero), jnp.where(first, zero, q2[:cells]),
                 jnp.where(first, q2[cells:], zero), jnp.where(first, zero, q2[cells:])], axis=0)
            row = i * rows + p * 2
            base = [((row + t) * ncol + c) * 9 for t in range(2)]
            s = []
            for j in range(3):
                kj = k_refs[c + j][0, pl.ds(off, 4 * cells), :]
                s.append(dot(kj, qbd, NT))
            tots = []
            for t in range(2):
                ls = slice(t * width, (t + 1) * width)
                m = None
                lws = {}
                for j in range(3):
                    for u in range(3):
                        lw = lw_ref[base[t] + j * 3 + u]
                        lws[j, u] = lw
                        blk = s[j][(t + u) * cells:(t + u + 1) * cells, ls]
                        pm = jnp.max(blk.reshape(cells // 8, 8, width), axis=0) + jnp.minimum(lw, 0.0)
                        m = pm if m is None else jnp.maximum(m, pm)
                m = jnp.max(m, axis=0, keepdims=True) * LOG2E
                tot = None
                for j in range(3):
                    for u in range(3):
                        blk = s[j][(t + u) * cells:(t + u + 1) * cells, ls]
                        e = jnp.exp2(blk * LOG2E - (m - lws[j, u]))
                        ps = jnp.sum(e.reshape(cells // 8, 8, width), axis=0)
                        tot = ps if tot is None else tot + ps
                        p_ref[c, j, (t + u) * cells:(t + u + 1) * cells, ls] = e.astype(bf16)
                tots.append(1.0 / jnp.sum(tot, axis=0, keepdims=True))
            o = None
            for j in range(3):
                vj = v_refs[c + j][0, :, pl.ds(off, 4 * cells)]
                d = dot(vj, p_ref[c, j])
                o = d if o is None else o + d
            mixed = []
            for t in range(2):
                ot = (o[:, t * width:(t + 1) * width] * tots[t]).T
                mixed.append(jnp.where(first, ot[:cells], ot[cells:]).astype(bf16))
            up = dot(jnp.concatenate(mixed, axis=0), wo)
            cu = cu_ref[pl.ds(row // 4, 1), :]
            out_ref[pl.ds(p * 2, 2), c] = (up + cu).astype(bf16).reshape(2, cells, width)
        return carry
    lax.fori_loop(0, rows // 2, pair_rows, 0)

def attend(lw, qs, ks, vs, wo, cu, lat, rows=8, unroll=1):
    ncol = len(qs)
    cells = HD
    width = wo.shape[0]
    n = rows * cells
    qspec = pl.BlockSpec((1, n, width), lambda i: (0, i, 0))
    kspec = pl.BlockSpec((pl.Element(1), pl.Element(n + 2 * cells), pl.Element(width)), lambda i: (0, i * n, 0))
    vspec = pl.BlockSpec((pl.Element(1), pl.Element(width), pl.Element(n + 2 * cells)), lambda i: (0, 0, i * n))
    return pl.pallas_call(
        functools.partial(attend_kernel, rows, ncol),
        grid=(lat // rows,),
        in_specs=[pl.BlockSpec(memory_space=pltpu.SMEM)] + [qspec] * ncol + [kspec] * (ncol + 2) + [vspec] * (ncol + 2)
        + [pl.BlockSpec(wo.shape, lambda i: (0, 0)), pl.BlockSpec(cu.shape, lambda i: (0, 0))],
        out_specs=pl.BlockSpec((rows, ncol, cells, width), lambda i: (i, 0, 0, 0)),
        out_shape=jax.ShapeDtypeStruct((lat, ncol, cells, width), bf16),
        scratch_shapes=[pltpu.VMEM((ncol, 3, 4 * cells, 2 * width), bf16)],
        name="attend",
    )(lw, *qs, *ks, *vs, wo, cu)


def pool_kernel(side, step_ref, freq_ref, weight_ref, tok_ref, part_ref, gain_ref):
    i = pl.program_id(0)
    rows, columns, cells, width = tok_ref.shape

    @pl.when(i == 0)
    def _():
        angles = step_ref[0].astype(f32) * freq_ref[...]
        features = jnp.concatenate([jnp.cos(angles), jnp.sin(angles)], axis=1).astype(bf16)
        gain_ref[...] = 1.0 + dot(features, weight_ref[...])

    gain = gain_ref[...][:1]
    for g in range(rows // side):
        x = tok_ref[g * side:(g + 1) * side].reshape(side * columns * cells, width)
        normed = normed_of(x, gain, None).astype(f32)
        total = jnp.sum(normed.reshape(-1, 8, width), axis=0)
        part_ref[pl.ds(i * (rows // side) + g, 1), :] = jnp.sum(total, axis=0, keepdims=True)

def pool(tokens, time_step, freqs, time_weight, rows=16):
    lat, columns, cells, width = tokens.shape
    side = POOL // TILE
    return pl.pallas_call(
        functools.partial(pool_kernel, side),
        grid=(lat // rows,),
        in_specs=[pl.BlockSpec(memory_space=pltpu.SMEM),
                  pl.BlockSpec(freqs.shape, lambda i: (0, 0)),
                  pl.BlockSpec(time_weight.shape, lambda i: (0, 0)),
                  pl.BlockSpec((rows, columns, cells, width), lambda i: (i, 0, 0, 0))],
        out_specs=[pl.BlockSpec((lat // side, width), lambda i: (0, 0)), pl.BlockSpec((8, width), lambda i: (0, 0))],
        out_shape=[jax.ShapeDtypeStruct((lat // side, width), f32), jax.ShapeDtypeStruct((8, width), f32)],
        name="pool",
    )(time_step, freqs, time_weight, tokens)

def coarse_kernel(pair, nblocks, *refs):
    blocks = refs[:nblocks]
    cin_ref, wq_ref, wk_ref, wv_ref, wo_ref, scale_ref, ones_ref, out_ref, coarse_ref = refs[nblocks:]
    g = pl.program_id(0)
    cell_rows, width = out_ref.shape

    @pl.when(g == 0)
    def _():
        parts = []
        for ref in blocks:
            value = ref[...]
            parts += [value[a * cell_rows:(a + 1) * cell_rows] for a in range(value.shape[0] // cell_rows)]
        pooled = []
        for a in range(0, len(parts), pair):
            total = parts[a]
            for b in range(1, pair):
                total = total + parts[a + b]
            pooled.append(total)
        pooled = (jnp.concatenate(pooled, axis=0) / (POOL * POOL)).astype(bf16)
        raw = dot(pooled, cin_ref[...])
        coarse_ref[...] = (raw * lax.rsqrt(jnp.mean(raw * raw, axis=-1, keepdims=True) + EPS)).astype(bf16)
        out_ref[...] = jnp.zeros_like(out_ref)

    coarse = coarse_ref[...]
    sub = wq_ref.shape[1]
    heads = sub // HD
    ones = ones_ref[...]
    lane_head = lax.broadcasted_iota(jnp.int32, (cell_rows, sub), 1) // HD
    q = dot(coarse[:cell_rows], wq_ref[...])
    q = (q * lax.rsqrt(block_sum(q * q, ones) + EPS) * scale_ref[...]).astype(bf16)
    k = dot(coarse, wk_ref[...])
    k = (k * lax.rsqrt(block_sum(k * k, ones) + EPS)).astype(bf16)
    v = dot(coarse, wv_ref[...]).astype(bf16)
    qbd = jnp.concatenate([jnp.where(lane_head == h, q, jnp.zeros_like(q)) for h in range(heads)], axis=0)
    s = dot(qbd, k, NT)
    e = jnp.exp(s - jnp.max(s, axis=-1, keepdims=True))
    o = dot(e.astype(bf16), v) / jnp.sum(e, axis=-1, keepdims=True)
    mixed = o[:cell_rows]
    for h in range(1, heads):
        mixed = jnp.where(lane_head == h, o[h * cell_rows:(h + 1) * cell_rows], mixed)
    out_ref[...] += dot(mixed.astype(bf16), wo_ref[...])

def coarse_level(blocks, coarse_input, coarse_project, coarse_scale, coarse_output, cell_rows, pair, sub=256):
    width, dc = coarse_input.shape
    steps = dc // sub
    ncells = sum(b.shape[0] for b in blocks) // pair
    ones = jnp.asarray(ones_block(sub, HD), bf16)
    scale = jnp.repeat(coarse_scale, HD)[None, :]
    whole = lambda a: pl.BlockSpec(a.shape, lambda g: (0,) * a.ndim)
    return pl.pallas_call(
        functools.partial(coarse_kernel, pair, len(blocks)),
        grid=(steps,),
        in_specs=[whole(b) for b in blocks] + [
            whole(coarse_input),
            pl.BlockSpec((dc, sub), lambda g: (0, g)),
            pl.BlockSpec((dc, sub), lambda g: (0, steps + g)),
            pl.BlockSpec((dc, sub), lambda g: (0, 2 * steps + g)),
            pl.BlockSpec((sub, width), lambda g: (g, 0)),
            pl.BlockSpec((1, sub), lambda g: (0, g)),
            whole(ones)],
        out_specs=pl.BlockSpec((cell_rows, width), lambda g: (0, 0)),
        out_shape=jax.ShapeDtypeStruct((cell_rows, width), f32),
        scratch_shapes=[pltpu.VMEM((ncells, dc), bf16)],
        name="coarse",
    )(*blocks, coarse_input, coarse_project, coarse_project, coarse_project, coarse_output, scale, ones)

def gather_stages(size, radix=4):
    stages, stride = [], 1
    while stride < size:
        count = min(radix, size // stride)
        stages.append((stride, count))
        stride *= count
    return stages

def gather_blocks(value, axis):
    size = lax.axis_size(axis)
    blocks = [value]
    for stride, count in gather_stages(size):
        held = blocks[0] if len(blocks) == 1 else jnp.concatenate(blocks, axis=0)
        blocks = [held] if len(blocks) == 1 else blocks
        for other in range(1, count):
            pairs = [(source, source ^ (other * stride)) for source in range(size)]
            blocks = blocks + [lax.ppermute(held, axis, pairs)]
    return blocks

def shards(tokens, neighbours, time_step, time_weight, fine_project, fine_output, fine_scale,
           coarse_input, coarse_project, coarse_scale, coarse_output):
    lat, columns, cells, width = tokens.shape
    size = lax.axis_size("lon")
    up = [(i, (i + 1) % size) for i in range(size)]
    down = [(j, i) for i, j in up]
    before = lax.ppermute(tokens[:, columns - 1:], "lon", up)
    after = lax.ppermute(tokens[:, :1], "lon", down)

    half = time_weight.shape[0] // 2
    freqs = jnp.asarray(np.exp(np.arange(half) * (-math.log(10000.0) / half))[None, :].repeat(8, 0), f32)
    part, gain8 = pool(tokens, time_step, freqs, time_weight)
    gain = gain8[:1]
    blocks = gather_blocks(part, "lon")

    step = neighbours // (columns * size) - jnp.arange(lat, dtype=jnp.int32)[:, None, None]
    near = step.reshape(lat, columns, 3, 1, 3) == jnp.arange(-1, 2, dtype=jnp.int32)[:, None]
    count = jnp.sum(near.astype(jnp.int32), axis=-1)
    log_count = jnp.where(count == 0, -1e30, jnp.where(count == 1, 0.0, jnp.where(count == 2, 1.0, math.log2(3.0))))
    lw = log_count.astype(f32).reshape(-1)

    ones = jnp.asarray(ones_block(width, HD), bf16)
    scale = jnp.repeat(fine_scale, HD)[None, :]
    wqk = fine_project[:, :2 * width]
    wvt = fine_project[:, 2 * width:].T
    q, k, vt = project(tokens, gain, wqk, wvt, ones, scale, True, rows=16)
    sides = [project(x, gain, wqk[:, width:], wvt, ones, scale, False, rows=16) for x in (before, after)]
    pad_k = lambda a: jnp.pad(a, ((0, 0), (cells, cells), (0, 0)))
    pad_v = lambda a: jnp.pad(a, ((0, 0), (0, 0), (cells, cells)))
    ks = [sides[0][0]] + [k[c:c + 1] for c in range(columns)] + [sides[1][0]]
    vs = [sides[0][1]] + [vt[c:c + 1] for c in range(columns)] + [sides[1][1]]
    side = POOL // TILE
    pair = POOL // (TILE * columns)
    cu = coarse_level(blocks, coarse_input, coarse_project, coarse_scale, coarse_output, lat // side, pair)
    return attend(lw, [q[c:c + 1] for c in range(columns)], [pad_k(a) for a in ks], [pad_v(a) for a in vs],
                  fine_output, cu, lat, rows=16)

def solution(mesh):
    return jax.shard_map(
        shards,
        mesh=mesh,
        in_specs=(P("group", "lon", None, None), P(None, "lon", None), P("group"),
                  P(), P(), P(), P(), P(), P(), P(), P()),
        out_specs=P("group", "lon", None, None),
        check_vma=False,
    )
```

time: 653 us -> 124 us (0.19); the launches traced: 645 us -> 123 us
  local copies, waits for them, and re-layouts: 301 us -> 29.1 us
  matrix products: 130 us -> 0 us
  other arithmetic: 123 us -> 0.14 us
  Pallas kernels: 0 us -> 81.3 us
  blocking collectives: 71.4 us -> 0 us
  loops' own time: 11.9 us -> 0 us
    dot_general x41 -> x0, matrix products: 117 us -> none  [the longest x16 52.3 us: local_attend(): jnp.einsum('tqhd,tkhd->thqk', query_heads, key_heads, preferred_element_t...]
    concatenate x18 -> x1, local copies, waits for them, and re-layouts: 89.7 us -> 0.59 us  [gather_blocks(): held = blocks[0] if len(blocks) == 1 else jnp.concatenate(blocks, axis=0)]
    while x208 -> x0, local copies, waits for them, and re-layouts: 82.1 us -> none
    pallas_call x0 -> x6, Pallas kernels: none -> 81.3 us  [the longest x1 51.3 us: attend(): pl.pallas_call(functools.partial(attend_kernel, rows, ncol), grid=(lat //...]
    slice x35 -> x7, local copies, waits for them, and re-layouts: 81.4 us -> 8.38 us  [the longest x1 3.14 us: shards(): q[c:c + 1]]
    all_gather x2 -> x0, blocking collectives: 71.4 us -> none  [the longest x1 51.1 us: shards(): lax.all_gather(cell_keys, 'lon', axis=0, tiled=True)]
    select_n x32 -> x1, other arithmetic: 70.1 us -> 0.01 us  [shards(): jnp.where(count == 0, -1e+30, jnp.where(count == 1, 0.0, jnp.where(count...]
    dynamic_slice x37 -> x0, local copies, waits for them, and re-layouts: 26.6 us -> none  [the longest x32 26.3 us: shards(): fine_mixed = lax.map(attend_block, (query_blocks, step_blocks, block_ids))]
  transfers between devices with their start and end apart: 4 -> 8, of which waited for: 0 -> 0; matrix products, arithmetic and copies ran while one was open for 5% -> 17% of each run, Pallas kernels for 0% -> 17%
where the time goes in v1:
time: 124 us; the launch traced here: 123 us
  Pallas kernels  81.3 us (66%)
  local copies, waits for them, and re-layouts  29.1 us (23%)
  starting transfers between devices  12 us (10%)
    pallas_call x1, Pallas kernels, attend(): pl.pallas_call(functools.partial(attend_kernel, rows, ncol), grid=(lat //...  51.3 us
    pallas_call x3, Pallas kernels, project(): pl.pallas_call(functools.partial(project_kernel, with_query, rows), grid=...  18.2 us
    pallas_call x1, Pallas kernels, coarse_level(): pl.pallas_call(functools.partial(coarse_kernel, pair, len(blocks)), grid=...  7.65 us
    ppermute x6, starting transfers between devices, gather_blocks(): blocks = blocks + [lax.ppermute(held, axis, pairs)]  7.53 us
    pad x4, local copies, waits for them, and re-layouts, shards(): pad_k = lambda a: jnp.pad(a, ((0, 0), (cells, cells), (0, 0)))  6.9 us
    pad x4, local copies, waits for them, and re-layouts, shards(): pad_v = lambda a: jnp.pad(a, ((0, 0), (0, 0), (cells, cells)))  5.6 us
    unnamed x38, local copies, waits for them, and re-layouts  5.21 us
    ppermute x1, starting transfers between devices, shards(): after = lax.ppermute(tokens[:, :1], 'lon', down)  4.5 us
  transfers between devices with their start and end apart: 8, of which 0 were waited for; matrix products, arithmetic and copies ran while one was open for 17% of the time, Pallas kernels for 17%

profile of v1, /device:TPU:0, one launch (start us, length us, event | category | flops | bytes accessed | tf_op | source)
XLA Modules:
  0.0 123.5 jit_solution(11900521480689099931)
XLA Ops:
  0.8 4.1 %pool.1 = (f32[16,128]{1,0:T(8,128)}, f32[8,128]{1,0:T(8,128)}) custom-call(s32[1]{0:T(128)S(6)} %copy.25.step_ref, f32[8,128]{1,0:T(8,128)} %constant.38.clone.freq_ref, bf16[256,128]{1,0:T(8,128)(2,1)} %weight_ref.1, bf16[64,2,64,128]{3,2,1,0:T(8,128)(2,1)} %tok_ref.3), custom_call_target="tpu_custom_call" | custom-call | tf_op jit(solution)/shard_map/pool/pallas_call | solution.py:186
  4.9 2.5 %collective-permute-start.4 = (f32[16,128]{1,0:T(8,128)}, f32[16,128]{1,0:T(8,128)S(1)}, u32[]{:S(2)}, u32[]{:S(2)}) collective-permute-start(f32[16,128]{1,0:T(8,128)} %get-tuple-element.22.refs_0_), channel_id=1, source_target_pairs={{0,3},{1,2},{2,1},{3,0},{4,7},{5,6},{6,5},{7,4},{8,11},{9,10},{10,... | collective-permute-start | bytes 24584 | tf_op jit(solution)/shard_map/ppermute | solution.py:280
  7.4 0.6 collective-permute-start.3
  8.0 1.6 %fusion.2 = (bf16[64,1,64,128]{3,2,1,0:T(8,128)(2,1)}, bf16[64,1,64,128]{3,2,1,0:T(8,128)(2,1)}) fusion(bf16[64,2,64,128]{3,2,1,0:T(8,128)(2,1)S(1)} %copy-done), kind=kLoop, calls=%fused_computation.16 | loop fusion | bytes 4194304 | tf_op jit(solution)/shard_map/slice | solution.py:290
  9.6 4.5 %collective-permute-start.1 = (bf16[64,1,64,128]{3,2,1,0:T(8,128)(2,1)}, bf16[64,1,64,128]{3,2,1,0:T(8,128)(2,1)}, u32[]{:S(2)}, u32[]{:S(2)}) collective-permute-start(bf16[64,1,64,128]{3,2,1,0:T(8,128)(2,1)} %get-tuple-element.25), channel_id=1, source_target_pairs={{1,0},{2,1},{3,2},{4,3},{5,4},{6,5},{7,6},{8,7},{9,8},{10,9},{11,1... | collective-permute-start | bytes 3145736 | tf_op jit(solution)/shard_map/ppermute | solution.py:290
  14.1 0.6 slice.39.wqk_ref
  14.7 0.6 fusion.5
  15.4 0.6 broadcast_in_dim_reshape.6.scale_ref
  16.0 1.2 slice.38.gain_ref
  17.2 0.7 copy.21
  17.9 9.0 %project.3 = (bf16[2,4096,128]{2,1,0:T(8,128)(2,1)}, bf16[2,4096,128]{2,1,0:T(8,128)(2,1)}, bf16[2,128,4096]{2,1,0:T(8,128)(2,1)}) custom-call(bf16[64,2,64,128]{3,2,1,0:T(8,128)(2,1)} %tok_ref.3, f32[1,128]{1,0:T(1,128)} %slice.38.gain_ref, bf16[128,256]{1,0:T(8,128)(2,1)} %slice.39.wqk_ref, bf16[128,128]{1,0:T(8,128)(2,1)} %bitcast.2, ...), custom_call_target="tpu_custom_call" | custom-call | tf_op jit(solution)/shard_map/project/pallas_call | solution.py:70
  26.9 3.1 %fusion.4 = (bf16[1,4096,128]{2,1,0:T(8,128)(2,1)}, bf16[1,4096,128]{2,1,0:T(8,128)(2,1)}) fusion(bf16[2,4096,128]{2,1,0:T(8,128)(2,1)} %get-tuple-element.15), kind=kLoop, calls=%fused_computation.18 | loop fusion | bytes 4194304 | tf_op jit(solution)/shard_map/slice | solution.py:317
  30.2 1.4 %copy-done.2 = bf16[2,128,4096]{2,1,0:T(8,128)(2,1)S(1)} copy-done((bf16[2,128,4096]{2,1,0:T(8,128)(2,1)S(1)}, bf16[2,128,4096]{2,1,0:T(8,128)(2,1)}, u32[]{:S(2)}) %copy-start.2) | copy-done | bytes 2097176
  31.6 1.1 fusion.1
  33.5 0.6 constant_dynamic-update-slice_fusion.2
  34.1 0.6 constant_dynamic-update-slice_fusion.1
  35.7 3.9 %collective-permute-start.5 = (f32[64,128]{1,0:T(8,128)}, f32[64,128]{1,0:T(8,128)S(1)}, u32[]{:S(2)}, u32[]{:S(2)}) collective-permute-start(f32[64,128]{1,0:T(8,128)} %constant_dynamic-update-slice_fusion), channel_id=1, source_target_pairs={{0,4},{1,5},{2,6},{3,7},{4,0},{5,1},{6,2},{7,3},{8,12},{9,13},{10,... | collective-permute-start | bytes 98312 | tf_op jit(solution)/shard_map/ppermute | solution.py:280
  39.8 0.7 broadcast_in_dim_reshape.7.refs_12_
  40.6 0.8 select_n.28.lw_ref
  41.4 1.0 pad.28.refs_4_
  42.5 1.1 pad.27.refs_3_
  43.6 1.4 %pad.32.refs_8_ = bf16[1,128,4224]{2,1,0:T(8,128)(2,1)} pad(bf16[1,128,4096]{2,1,0:T(8,128)(2,1)S(1)} %copy-done.1, bf16[]{:T(256)} %constant.37.clone.1), padding=0_0x0_0x64_64 | pad | bytes 2129922 | tf_op jit(solution)/shard_map/jit(_pad)/pad | solution.py:311
  44.9 1.4 %pad.31.refs_7_ = bf16[1,128,4224]{2,1,0:T(8,128)(2,1)} pad(bf16[1,128,4096]{2,1,0:T(8,128)(2,1)S(1)} %get-tuple-element.24, bf16[]{:T(256)} %constant.37.clone.1), padding=0_0x0_0x64_64 | pad | bytes 2129922 | tf_op jit(solution)/shard_map/jit(_pad)/pad | solution.py:311
  47.0 0.6 copy-done.13
  47.6 7.6 %coarse.1.refs_11_ = f32[16,128]{1,0:T(8,128)} custom-call(f32[16,128]{1,0:T(8,128)} %get-tuple-element.22.refs_0_, f32[16,128]{1,0:T(8,128)} %copy-done.10, f32[16,128]{1,0:T(8,128)} %copy-done.9, f32[16,128]{1,0:T(8,128)} %copy-done.8, f32[64,128]{1,0:T(8,128)} %copy-done.13, f32[64,128]{1,0:T(8,128)} %copy-done.12, f32[64,128]{1,0:T(8,128)} %copy-done.11, ...), custom_call_target="tpu_custom_call" | custom-call | tf_op jit(solution)/shard_map/coarse/pallas_call | solution.py:247
  55.2 4.6 %project.5 = (bf16[1,4096,128]{2,1,0:T(8,128)(2,1)}, bf16[1,128,4096]{2,1,0:T(8,128)(2,1)}) custom-call(bf16[64,1,64,128]{3,2,1,0:T(8,128)(2,1)} %collective-permute-done.1.tok_ref, f32[1,128]{1,0:T(1,128)} %slice.38.gain_ref, bf16[128,128]{1,0:T(8,128)(2,1)} %get-tuple-element.31.wqk_ref, bf16[128,128]{1,0:T(8,128)(2,1)} %bitcast.3, ...), custom_call_target="tpu_custom_call" | custom-call | tf_op jit(solution)/shard_map/project/pallas_call | solution.py:70
  59.9 2.3 %pad.29.refs_5_ = bf16[1,4224,128]{2,1,0:T(8,128)(2,1)} pad(bf16[1,4096,128]{2,1,0:T(8,128)(2,1)} %get-tuple-element.18, bf16[]{:T(256)} %constant.37.clone.1), padding=0_0x64_64x0_0 | pad | bytes 2129922 | tf_op jit(solution)/shard_map/jit(_pad)/pad | solution.py:310
  62.2 4.6 %project.4 = (bf16[1,4096,128]{2,1,0:T(8,128)(2,1)}, bf16[1,128,4096]{2,1,0:T(8,128)(2,1)}) custom-call(bf16[64,1,64,128]{3,2,1,0:T(8,128)(2,1)} %collective-permute-done.tok_ref, f32[1,128]{1,0:T(1,128)} %slice.38.gain_ref, bf16[128,128]{1,0:T(8,128)(2,1)} %get-tuple-element.31.wqk_ref, bf16[128,128]{1,0:T(8,128)(2,1)} %bitcast.4, ...), custom_call_target="tpu_custom_call" | custom-call | tf_op jit(solution)/shard_map/project/pallas_call | solution.py:70
  66.8 2.5 %pad.26.refs_2_ = bf16[1,4224,128]{2,1,0:T(8,128)(2,1)} pad(bf16[1,4096,128]{2,1,0:T(8,128)(2,1)} %get-tuple-element.16, bf16[]{:T(256)} %constant.37.clone.1), padding=0_0x64_64x0_0 | pad | bytes 2129922 | tf_op jit(solution)/shard_map/jit(_pad)/pad | solution.py:310
  69.3 1.4 %pad.30.refs_6_ = bf16[1,128,4224]{2,1,0:T(8,128)(2,1)} pad(bf16[1,128,4096]{2,1,0:T(8,128)(2,1)S(1)} %copy-done.5, bf16[]{:T(256)} %constant.37.clone.1), padding=0_0x0_0x64_64 | pad | bytes 2129922 | tf_op jit(solution)/shard_map/jit(_pad)/pad | solution.py:311
  70.7 1.5 %pad.33.refs_9_ = bf16[1,128,4224]{2,1,0:T(8,128)(2,1)} pad(bf16[1,128,4096]{2,1,0:T(8,128)(2,1)S(1)} %copy-done.4, bf16[]{:T(256)} %constant.37.clone.1), padding=0_0x0_0x64_64 | pad | bytes 2129922 | tf_op jit(solution)/shard_map/jit(_pad)/pad | solution.py:311
  72.2 51.3 %attend.1 = bf16[64,2,64,128]{3,2,1,0:T(8,128)(2,1)} custom-call(f32[1152]{0:T(1024)} %select_n.28.lw_ref, bf16[1,4096,128]{2,1,0:T(8,128)(2,1)} %get-tuple-element.30.refs_0_, bf16[1,4096,128]{2,1,0:T(8,128)(2,1)} %get-tuple-element.29.refs_1_, bf16[1,4224,128]{2,1,0:T(8,128)(2,1)} %pad.26.refs_2_, bf16[1,4224,128]{2,1,0:T(8,128)(2,1)} %pad.27.refs_3_, ...), custom_call_target="tpu_custom_call" | custom-call | tf_op jit(solution)/shard_map/attend/pallas_call | solution.py:154
  (54 shorter events, 3.0 us)
Async XLA Ops:
  0.0 8.0 %copy-start = (bf16[64,2,64,128]{3,2,1,0:T(8,128)(2,1)S(1)}, bf16[64,2,64,128]{3,2,1,0:T(8,128)(2,1)}, u32[]{:S(2)}) copy-start(bf16[64,2,64,128]{3,2,1,0:T(8,128)(2,1)} %tok_ref.3) | copy-start | bytes 6291460
  4.9 9.2 %copy-start.6 = (bf16[128,384]{1,0:T(8,128)(2,1)S(1)}, bf16[128,384]{1,0:T(8,128)(2,1)}, u32[]{:S(2)}) copy-start(bf16[128,384]{1,0:T(8,128)(2,1)} %param.18) | copy-start | bytes 294916
  4.9 10.5 %copy-start.16 = (f32[2]{0:T(128)S(1)}, f32[2]{0:T(128)}, u32[]{:S(2)}) copy-start(f32[2]{0:T(128)} %param.20) | copy-start | bytes 28
  4.9 29.8 %collective-permute-start.4 = (f32[16,128]{1,0:T(8,128)}, f32[16,128]{1,0:T(8,128)S(1)}, u32[]{:S(2)}, u32[]{:S(2)}) collective-permute-start(f32[16,128]{1,0:T(8,128)} %get-tuple-element.22.refs_0_), channel_id=1, source_target_pairs={{0,3},{1,2},{2,1},{3,0},{4,7},{5,6},{6,5},{7,4},{8,11},{9,10},{10,... | collective-permute-start | bytes 24584 | tf_op jit(solution)/shard_map/ppermute | solution.py:280
  7.4 26.7 %collective-permute-start.3 = (f32[16,128]{1,0:T(8,128)}, f32[16,128]{1,0:T(8,128)S(1)}, u32[]{:S(2)}, u32[]{:S(2)}) collective-permute-start(f32[16,128]{1,0:T(8,128)} %get-tuple-element.22.refs_0_), channel_id=1, source_target_pairs={{0,2},{1,3},{2,0},{3,1},{4,6},{5,7},{6,4},{7,5},{8,10},{9,11},{10,... | collective-permute-start | bytes 24584 | tf_op jit(solution)/shard_map/ppermute | solution.py:280
  8.0 25.5 %collective-permute-start.2 = (f32[16,128]{1,0:T(8,128)}, f32[16,128]{1,0:T(8,128)S(1)}, u32[]{:S(2)}, u32[]{:S(2)}) collective-permute-start(f32[16,128]{1,0:T(8,128)} %get-tuple-element.22.refs_0_), channel_id=1, source_target_pairs={{0,1},{1,0},{2,3},{3,2},{4,5},{5,4},{6,7},{7,6},{8,9},{9,8},{10,11... | collective-permute-start | bytes 24584 | tf_op jit(solution)/shard_map/ppermute | solution.py:280
  9.6 45.6 %collective-permute-start.1 = (bf16[64,1,64,128]{3,2,1,0:T(8,128)(2,1)}, bf16[64,1,64,128]{3,2,1,0:T(8,128)(2,1)}, u32[]{:S(2)}, u32[]{:S(2)}) collective-permute-start(bf16[64,1,64,128]{3,2,1,0:T(8,128)(2,1)} %get-tuple-element.25), channel_id=1, source_target_pairs={{1,0},{2,1},{3,2},{4,3},{5,4},{6,5},{7,6},{8,7},{9,8},{10,9},{11,1... | collective-permute-start | bytes 3145736 | tf_op jit(solution)/shard_map/ppermute | solution.py:290
  14.1 48.1 %collective-permute-start = (bf16[64,1,64,128]{3,2,1,0:T(8,128)(2,1)}, bf16[64,1,64,128]{3,2,1,0:T(8,128)(2,1)}, u32[]{:S(2)}, u32[]{:S(2)}) collective-permute-start(bf16[64,1,64,128]{3,2,1,0:T(8,128)(2,1)} %get-tuple-element.26), channel_id=1, source_target_pairs={{0,1},{1,2},{2,3},{3,4},{4,5},{5,6},{6,7},{7,8},{8,9},{9,10},{10,1... | collective-permute-start | bytes 3145736 | tf_op jit(solution)/shard_map/ppermute | solution.py:289
  26.9 3.1 %copy-start.3 = (bf16[2,4096,128]{2,1,0:T(8,128)(2,1)S(1)}, bf16[2,4096,128]{2,1,0:T(8,128)(2,1)}, u32[]{:S(2)}) copy-start(bf16[2,4096,128]{2,1,0:T(8,128)(2,1)} %get-tuple-element.17) | copy-start | bytes 6291460
  30.0 1.6 %copy-start.2 = (bf16[2,128,4096]{2,1,0:T(8,128)(2,1)S(1)}, bf16[2,128,4096]{2,1,0:T(8,128)(2,1)}, u32[]{:S(2)}) copy-start(bf16[2,128,4096]{2,1,0:T(8,128)(2,1)} %get-tuple-element.20) | copy-start | bytes 6291460
  31.6 1.1 copy-start.14
  31.6 1.2 %copy-start.7 = (f32[16,128]{1,0:T(8,128)S(1)}, f32[16,128]{1,0:T(8,128)}, u32[]{:S(2)}) copy-start(f32[16,128]{1,0:T(8,128)} %get-tuple-element.22.refs_0_) | copy-start | bytes 24580
  31.6 8.1 %copy-start.15 = (f32[16]{0:T(128)S(1)}, f32[16]{0:T(128)}, u32[]{:S(2)}) copy-start(f32[16]{0:T(128)} %param.23) | copy-start | bytes 196
  33.5 10.1 %copy-start.10 = (f32[16,128]{1,0:T(8,128)}, f32[16,128]{1,0:T(8,128)S(1)}, u32[]{:S(2)}) copy-start(f32[16,128]{1,0:T(8,128)S(1)} %collective-permute-done.2.refs_1_) | copy-start | bytes 24580
  34.1 9.5 %copy-start.9 = (f32[16,128]{1,0:T(8,128)}, f32[16,128]{1,0:T(8,128)S(1)}, u32[]{:S(2)}) copy-start(f32[16,128]{1,0:T(8,128)S(1)} %collective-permute-done.3.refs_2_) | copy-start | bytes 24580
  34.7 8.9 %copy-start.8 = (f32[16,128]{1,0:T(8,128)}, f32[16,128]{1,0:T(8,128)S(1)}, u32[]{:S(2)}) copy-start(f32[16,128]{1,0:T(8,128)S(1)} %collective-permute-done.4.refs_3_) | copy-start | bytes 24580
  35.3 11.1 %collective-permute-start.7 = (f32[64,128]{1,0:T(8,128)}, f32[64,128]{1,0:T(8,128)S(1)}, u32[]{:S(2)}, u32[]{:S(2)}) collective-permute-start(f32[64,128]{1,0:T(8,128)} %constant_dynamic-update-slice_fusion), channel_id=1, source_target_pairs={{0,12},{1,13},{2,14},{3,15},{4,8},{5,9},{6,10},{7,11},{8,4},{9,5},... | collective-permute-start | bytes 98312 | tf_op jit(solution)/shard_map/ppermute | solution.py:280
  35.7 10.6 %collective-permute-start.6 = (f32[64,128]{1,0:T(8,128)}, f32[64,128]{1,0:T(8,128)S(1)}, u32[]{:S(2)}, u32[]{:S(2)}) collective-permute-start(f32[64,128]{1,0:T(8,128)} %constant_dynamic-update-slice_fusion), channel_id=1, source_target_pairs={{0,8},{1,9},{2,10},{3,11},{4,12},{5,13},{6,14},{7,15},{8,0},{9,1},... | collective-permute-start | bytes 98312 | tf_op jit(solution)/shard_map/ppermute | solution.py:280
  35.7 10.6 %collective-permute-start.5 = (f32[64,128]{1,0:T(8,128)}, f32[64,128]{1,0:T(8,128)S(1)}, u32[]{:S(2)}, u32[]{:S(2)}) collective-permute-start(f32[64,128]{1,0:T(8,128)} %constant_dynamic-update-slice_fusion), channel_id=1, source_target_pairs={{0,4},{1,5},{2,6},{3,7},{4,0},{5,1},{6,2},{7,3},{8,12},{9,13},{10,... | collective-permute-start | bytes 98312 | tf_op jit(solution)/shard_map/ppermute | solution.py:280
  41.4 2.1 %copy-start.1 = (bf16[1,128,4096]{2,1,0:T(8,128)(2,1)S(1)}, bf16[1,128,4096]{2,1,0:T(8,128)(2,1)}, u32[]{:S(2)}) copy-start(bf16[1,128,4096]{2,1,0:T(8,128)(2,1)} %get-tuple-element.23) | copy-start | bytes 3145732
  46.3 0.6 copy-start.11
  46.3 0.6 copy-start.12
  47.0 0.6 copy-start.13
  66.8 2.5 %copy-start.5 = (bf16[1,128,4096]{2,1,0:T(8,128)(2,1)S(1)}, bf16[1,128,4096]{2,1,0:T(8,128)(2,1)}, u32[]{:S(2)}) copy-start(bf16[1,128,4096]{2,1,0:T(8,128)(2,1)} %get-tuple-element.19) | copy-start | bytes 3145732
  66.8 3.9 %copy-start.4 = (bf16[1,128,4096]{2,1,0:T(8,128)(2,1)S(1)}, bf16[1,128,4096]{2,1,0:T(8,128)(2,1)}, u32[]{:S(2)}) copy-start(bf16[1,128,4096]{2,1,0:T(8,128)(2,1)} %get-tuple-element.21) | copy-start | bytes 3145732

commit v2 on v1

v2 whole, which is shorter than its diff:
```python
import functools
import math

import jax
import jax.numpy as jnp
import numpy as np
from jax import lax
from jax.experimental import pallas as pl
from jax.experimental.pallas import tpu as pltpu
from jax.sharding import PartitionSpec as P

HD = 64
TILE = 8
POOL = 32
EPS = 1e-6
LOG2E = math.log2(math.e)
SIDE = POOL // TILE
bf16, f32 = jnp.bfloat16, jnp.float32
NT = (((1,), (1,)), ((), ()))
NN = (((1,), (0,)), ((), ()))
SMEM = pl.BlockSpec(memory_space=pltpu.SMEM)
ANY = pl.BlockSpec(memory_space=pl.ANY)


def dot(a, b, dims=NN):
    return lax.dot_general(a, b, dims, preferred_element_type=f32)


def whole(a):
    return pl.BlockSpec(a.shape, lambda i: (0,) * a.ndim)


def ones_block(width, size):
    blocks = np.kron(np.eye(width // size), np.ones((size, size)))
    return jnp.asarray(np.concatenate([blocks, blocks], axis=0), bf16)


def block_sum(values, ones):
    high = values.astype(bf16)
    low = (values - high.astype(f32)).astype(bf16)
    return dot(jnp.concatenate([high, low], axis=1), ones)


def head_scales(scale_ref, start, width):
    head = lax.broadcasted_iota(jnp.int32, (1, width), 1) // HD
    out = jnp.zeros((1, width), f32)
    for h in range(width // HD):
        out = jnp.where(head == h, scale_ref[start + h], out)
    return out


def normed_of(x, gain):
    v = x.astype(f32)
    mean = jnp.mean(v * v, axis=-1, keepdims=True)
    return (v * lax.rsqrt(mean + EPS) * gain).astype(bf16)


def edges_kernel(tok_ref, first_ref, last_ref, sem):
    columns = tok_ref.shape[1]
    copies = [
        pltpu.make_async_copy(tok_ref.at[:, pl.ds(columns - 1, 1)], last_ref, sem.at[0]),
        pltpu.make_async_copy(tok_ref.at[:, pl.ds(0, 1)], first_ref, sem.at[1]),
    ]
    for copy in copies:
        copy.start()
    for copy in copies:
        copy.wait()


def edges(tokens):
    lat, _, cells, width = tokens.shape
    shape = jax.ShapeDtypeStruct((lat, 1, cells, width), tokens.dtype)
    return pl.pallas_call(
        edges_kernel,
        in_specs=[ANY],
        out_specs=[ANY, ANY],
        out_shape=[shape, shape],
        scratch_shapes=[pltpu.SemaphoreType.DMA((2,))],
        name="edges",
    )(tokens)


def pool_kernel(step_ref, freq_ref, weight_ref, tok_ref, part_ref, gain_ref):
    i = pl.program_id(0)
    rows, columns, cells, width = tok_ref.shape

    @pl.when(i == 0)
    def _():
        angles = step_ref[0].astype(f32) * freq_ref[...]
        features = jnp.concatenate([jnp.cos(angles), jnp.sin(angles)], axis=1).astype(bf16)
        gain_ref[...] = 1.0 + dot(features, weight_ref[...])

    gain = gain_ref[:1, :]
    for g in range(rows // SIDE):
        x = tok_ref[g * SIDE:(g + 1) * SIDE].reshape(SIDE * columns * cells, width)
        normed = normed_of(x, gain).astype(f32)
        total = jnp.sum(normed.reshape(-1, 8, width), axis=0)
        part_ref[pl.ds(i * (rows // SIDE) + g, 1), :] = jnp.sum(total, axis=0, keepdims=True)


def pool(tokens, time_step, time_weight, rows=16):
    lat, columns, cells, width = tokens.shape
    half = time_weight.shape[0] // 2
    freqs = np.exp(np.arange(half) * (-math.log(10000.0) / half))
    freqs = jnp.asarray(np.tile(freqs[None, :], (8, 1)), f32)
    shapes = [jax.ShapeDtypeStruct((lat // SIDE, width), f32), jax.ShapeDtypeStruct((8, width), f32)]
    return pl.pallas_call(
        pool_kernel,
        grid=(lat // rows,),
        in_specs=[SMEM, whole(freqs), whole(time_weight),
                  pl.BlockSpec((rows, columns, cells, width), lambda i: (i, 0, 0, 0))],
        out_specs=[whole(s) for s in shapes],
        out_shape=shapes,
        name="pool",
    )(time_step, freqs, time_weight, tokens)


def join_kernel(run, *refs):
    blocks, out_ref = refs[:-1], refs[-1]
    size = blocks[0].shape[0]
    for a in range(0, len(blocks), run):
        total = blocks[a][...]
        for b in range(1, run):
            total = total + blocks[a + b][...]
        out_ref[a // run * size:(a // run + 1) * size, :] = total


def join(blocks, run):
    size, width = blocks[0].shape
    shape = jax.ShapeDtypeStruct((len(blocks) // run * size, width), f32)
    return pl.pallas_call(functools.partial(join_kernel, run), out_shape=shape, name="join")(*blocks)


def gather_cells(part, axis, run):
    size = lax.axis_size(axis)
    held, blocks, stride = part, [part], 1
    while stride < size:
        count = min(4, size // stride)
        blocks = [held]
        for other in range(1, count):
            pairs = [(source, source ^ (other * stride)) for source in range(size)]
            blocks.append(lax.ppermute(held, axis, pairs))
        stride *= count
        if stride < size or run > 1:
            held = join(blocks, run)
            blocks, run = [held], 1
    return blocks


def project_kernel(with_query, rows, scale_ref, tok_ref, gain_ref, w_ref, ones_ref, *refs):
    outs, carry_ref = refs[:-1], refs[-1]
    k_ref, v_ref = outs[-2:]
    lat, _, cells, width = tok_ref.shape
    n = rows * cells
    ones = ones_ref[...]
    gain = gain_ref[:1, :]
    w = w_ref[...] if with_query else w_ref[:, width:]
    base = w.shape[1] - 2 * width
    zero = jnp.zeros((cells, width), bf16)
    k_ref[:cells, :] = zero
    k_ref[(lat + 1) * cells:, :] = zero
    carry_ref[...] = jnp.zeros_like(carry_ref)
    if with_query:
        scale = head_scales(scale_ref, 0, width)

    def chunk(i, carry):
        normed = normed_of(tok_ref[pl.ds(i * rows, rows), 0].reshape(n, width), gain)
        off = pl.multiple_of(i * n, n)
        out = dot(normed, w)
        if with_query:
            q = out[:, :width]
            outs[0][pl.ds(off, n), :] = (q * lax.rsqrt(block_sum(q * q, ones) + EPS) * scale).astype(bf16)
        k = out[:, base:base + width]
        k = k * lax.rsqrt(block_sum(k * k, ones) + EPS)
        k_ref[pl.ds(pl.multiple_of(off + cells, cells), n), :] = k.astype(bf16)
        v = jnp.concatenate([carry_ref[...], out[:, base + width:]], axis=0)
        for b in range(rows // 2):
            v_ref[i * (rows // 2) + b] = v[b * 2 * cells:(b + 1) * 2 * cells].T.astype(bf16)
        carry_ref[...] = v[n:]
        return carry

    lax.fori_loop(0, lat // rows, chunk, 0)
    last = jnp.concatenate([carry_ref[...], jnp.zeros_like(carry_ref)], axis=0)
    v_ref[lat // 2] = last.T.astype(bf16)


def project(tokens, column, gain, weights, ones, scale, with_query, rows=16):
    lat, _, cells, width = tokens.shape
    shapes = [jax.ShapeDtypeStruct(((lat + 2) * cells, width), bf16),
              jax.ShapeDtypeStruct((lat // 2 + 1, width, 2 * cells), bf16)]
    if with_query:
        shapes = [jax.ShapeDtypeStruct((lat * cells, width), bf16)] + shapes
    return pl.pallas_call(
        functools.partial(project_kernel, with_query, rows),
        grid=(1,),
        in_specs=[SMEM, pl.BlockSpec((lat, 1, cells, width), lambda i: (0, column, 0, 0)),
                  whole(gain), whole(weights), whole(ones)],
        out_specs=[whole(s) for s in shapes],
        out_shape=shapes,
        scratch_shapes=[pltpu.VMEM((cells, width), f32)],
        name="project",
    )(scale, tokens, gain, weights, ones)


def coarse_kernel(nblocks, scale_ref, *refs):
    blocks = refs[:nblocks]
    cin_ref, wq_ref, wk_ref, wv_ref, wo_ref, ones_ref, out_ref, coarse_ref = refs[nblocks:]
    g = pl.program_id(0)
    cell_rows, width = out_ref.shape

    @pl.when(g == 0)
    def _():
        pooled = jnp.concatenate([ref[...] for ref in blocks], axis=0)
        raw = dot((pooled / (POOL * POOL)).astype(bf16), cin_ref[...])
        coarse_ref[...] = (raw * lax.rsqrt(jnp.mean(raw * raw, axis=-1, keepdims=True) + EPS)).astype(bf16)
        out_ref[...] = jnp.zeros_like(out_ref)

    coarse = coarse_ref[...]
    sub = wq_ref.shape[1]
    heads = sub // HD
    ones = ones_ref[...]
    lane_head = lax.broadcasted_iota(jnp.int32, (cell_rows, sub), 1) // HD
    q = dot(coarse[:cell_rows], wq_ref[...])
    q = q * lax.rsqrt(block_sum(q * q, ones) + EPS) * head_scales(scale_ref, g * heads, sub)
    q = q.astype(bf16)
    k = dot(coarse, wk_ref[...])
    k = (k * lax.rsqrt(block_sum(k * k, ones) + EPS)).astype(bf16)
    v = dot(coarse, wv_ref[...]).astype(bf16)
    qbd = jnp.concatenate([jnp.where(lane_head == h, q, jnp.zeros_like(q)) for h in range(heads)], axis=0)
    s = dot(qbd, k, NT)
    e = jnp.exp(s - jnp.max(s, axis=-1, keepdims=True))
    o = dot(e.astype(bf16), v) / jnp.sum(e, axis=-1, keepdims=True)
    mixed = o[:cell_rows]
    for h in range(1, heads):
        mixed = jnp.where(lane_head == h, o[h * cell_rows:(h + 1) * cell_rows], mixed)
    out_ref[...] += dot(mixed.astype(bf16), wo_ref[...])


def coarse_level(blocks, coarse_input, coarse_project, coarse_scale, coarse_output, cell_rows, sub=256):
    width, dc = coarse_input.shape
    steps = dc // sub
    cells = sum(b.shape[0] for b in blocks)
    ones = ones_block(sub, HD)
    third = lambda t: pl.BlockSpec((dc, sub), lambda g: (0, t * steps + g))
    return pl.pallas_call(
        functools.partial(coarse_kernel, len(blocks)),
        grid=(steps,),
        in_specs=[SMEM] + [whole(b) for b in blocks]
        + [whole(coarse_input), third(0), third(1), third(2), pl.BlockSpec((sub, width), lambda g: (g, 0)), whole(ones)],
        out_specs=pl.BlockSpec((cell_rows, width), lambda g: (0, 0)),
        out_shape=jax.ShapeDtypeStruct((cell_rows, width), f32),
        scratch_shapes=[pltpu.VMEM((cells, dc), bf16)],
        name="coarse",
    )(coarse_scale, *blocks, coarse_input, coarse_project, coarse_project, coarse_project, coarse_output, ones)


def attend_kernel(rows, ncol, total_columns, near_ref, log_ref, *refs):
    q_refs = refs[:ncol]
    k_refs = refs[ncol:2 * ncol + 2]
    v_refs = refs[2 * ncol + 2:3 * ncol + 4]
    wo_ref, cu_ref, out_ref = refs[3 * ncol + 4:3 * ncol + 7]
    s_refs, m_refs, p_refs, lw_refs = (refs[3 * ncol + 7 + a * ncol:3 * ncol + 7 + (a + 1) * ncol] for a in range(4))
    i = pl.program_id(0)
    _, _, cells, width = out_ref.shape
    pairs = rows // 2
    span, reach = 4 * cells, 3 * cells

    @pl.when(i == 0)
    def _():
        for c in range(ncol):
            p_refs[c][...] = jnp.zeros_like(p_refs[c])

    first = lax.broadcasted_iota(jnp.int32, (cells, width), 1) < HD
    wo = wo_ref[...]
    zero = jnp.zeros((cells, width), bf16)

    def scores(p, c):
        off = pl.multiple_of(p * 2 * cells, 2 * cells)
        q2 = q_refs[c][pl.ds(off, 2 * cells), :]
        q0, q1 = q2[:cells], q2[cells:]
        left = jnp.concatenate([jnp.where(first, q0, zero), jnp.where(first, zero, q0), zero, zero], axis=0)
        right = jnp.concatenate([zero, zero, jnp.where(first, q1, zero), jnp.where(first, zero, q1)], axis=0)
        queries = jnp.concatenate([left, right], axis=1)
        largest = [None, None]
        for j in range(3):
            k0 = k_refs[c + j][pl.ds(off, reach), :]
            k1 = k_refs[c + j][pl.ds(pl.multiple_of(off + cells, cells), reach), :]
            s = dot(jnp.concatenate([k0, k1], axis=1), queries, NT)
            s_refs[c][j * reach:(j + 1) * reach, :] = s
            for t in range(2):
                row = i * rows + p * 2 + t
                steps = [near_ref[(row * ncol + c) * 9 + j * 3 + a] // total_columns - row for a in range(3)]
                below = sum((x < 0).astype(jnp.int32) for x in steps)
                above = sum((x > 0).astype(jnp.int32) for x in steps)
                for u, count in enumerate((below, 3 - below - above, above)):
                    log_count = log_ref[count]
                    lw_refs[c][(t * 3 + j) * 3 + u] = log_count
                    part = s[u * cells:(u + 1) * cells, t * width:(t + 1) * width]
                    part = jnp.max(part.reshape(cells // 8, 8, width), axis=0) + jnp.minimum(log_count, 0.0)
                    largest[t] = part if largest[t] is None else jnp.maximum(largest[t], part)
            if j == 2:
                for t in range(2):
                    top = jnp.max(largest[t], axis=0, keepdims=True) * LOG2E
                    m_refs[c][t * 8:(t + 1) * 8, :] = jnp.broadcast_to(top, (8, width))
            yield

    def soften(p, c):
        totals = [None, None]
        for j in range(3):
            for t in range(2):
                top = m_refs[c][t * 8:(t + 1) * 8, :]
                for u in range(3):
                    shift = top - lw_refs[c][(t * 3 + j) * 3 + u]
                    at = j * reach + u * cells
                    part = s_refs[c][at:at + cells, t * width:(t + 1) * width].reshape(cells // 8, 8, width)
                    raised = jnp.exp2(part * LOG2E - shift[None])
                    part = jnp.sum(raised, axis=0)
                    totals[t] = part if totals[t] is None else totals[t] + part
                    at = j * span + (t + u) * cells
                    p_refs[c][t, at:at + cells, :] = raised.reshape(cells, width).astype(bf16)
                if j == 2:
                    inverse = 1.0 / jnp.sum(totals[t], axis=0, keepdims=True)
                    m_refs[c][16 + t * 8:24 + t * 8, :] = jnp.broadcast_to(inverse, (8, width))
            yield

    def output(p, c):
        v = jnp.concatenate([v_refs[c + j][p + h] for j in range(3) for h in range(2)], axis=1)
        o = dot(v, jnp.concatenate([p_refs[c][0], p_refs[c][1]], axis=1))
        yield
        mixed = []
        for t in range(2):
            inverse = m_refs[c][16 + t * 8:24 + t * 8, :]
            part = o[:, t * width:(t + 1) * width].reshape(width // 8, 8, width) * inverse[None]
            part = part.reshape(width, width).T
            mixed.append(jnp.where(first, part[:cells], part[cells:]).astype(bf16))
        yield
        up = dot(jnp.concatenate(mixed, axis=0), wo)
        cu = cu_ref[pl.ds((i * rows + p * 2) // SIDE, 1), :]
        out_ref[pl.ds(p * 2, 2), c] = (up + cu).astype(bf16).reshape(2, cells, width)
        yield

    def together(*stages):
        for _ in range(3):
            for stage in stages:
                next(stage)

    together(*[scores(0, c) for c in range(ncol)])

    def body(p, carry):
        ahead, behind = jnp.minimum(p + 1, pairs - 1), jnp.maximum(p - 1, 0)
        for c in range(ncol):
            together(output(behind, c), soften(p, c), scores(ahead, c))
        return carry

    lax.fori_loop(0, pairs, body, 0)
    together(*[output(pairs - 1, c) for c in range(ncol)])


def attend(near, total_columns, qs, ks, vs, wo, cu, lat, cells, rows=16):
    ncol = len(qs)
    width = wo.shape[0]
    n = rows * cells
    logs = jnp.asarray([-1e30, 0.0, 1.0, math.log2(3.0)], f32)
    qspec = pl.BlockSpec((n, width), lambda i: (i, 0))
    kspec = pl.BlockSpec((pl.Element(n + 2 * cells), pl.Element(width)), lambda i: (i * n, 0))
    vspec = pl.BlockSpec((pl.Element(rows // 2 + 1), pl.Element(width), pl.Element(2 * cells)),
                         lambda i: (i * (rows // 2), 0, 0))
    return pl.pallas_call(
        functools.partial(attend_kernel, rows, ncol, total_columns),
        grid=(lat // rows,),
        in_specs=[SMEM, SMEM] + [qspec] * ncol + [kspec] * (ncol + 2) + [vspec] * (ncol + 2) + [whole(wo), whole(cu)],
        out_specs=pl.BlockSpec((rows, ncol, cells, width), lambda i: (i, 0, 0, 0)),
        out_shape=jax.ShapeDtypeStruct((lat, ncol, cells, width), bf16),
        scratch_shapes=[pltpu.VMEM((9 * cells, 2 * width), f32) for _ in range(ncol)]
        + [pltpu.VMEM((32, width), f32) for _ in range(ncol)]
        + [pltpu.VMEM((2, 12 * cells, width), bf16) for _ in range(ncol)]
        + [pltpu.SMEM((18,), f32) for _ in range(ncol)],
        name="attend",
    )(near, logs, *qs, *ks, *vs, wo, cu)


def shards(tokens, neighbours, time_step, time_weight, fine_project, fine_output, fine_scale,
           coarse_input, coarse_project, coarse_scale, coarse_output):
    lat, columns, cells, width = tokens.shape
    size = lax.axis_size("lon")
    up = [(i, (i + 1) % size) for i in range(size)]
    down = [(j, i) for i, j in up]
    first, last = edges(tokens)
    before = lax.ppermute(last, "lon", up)
    after = lax.ppermute(first, "lon", down)
    part, gain = pool(tokens, time_step, time_weight)
    blocks = gather_cells(part, "lon", POOL // (TILE * columns))
    ones = ones_block(width, HD)
    own = [project(tokens, c, gain, fine_project, ones, fine_scale, True) for c in range(columns)]
    cu = coarse_level(blocks, coarse_input, coarse_project, coarse_scale, coarse_output, lat // SIDE)
    sides = [project(x, 0, gain, fine_project, ones, fine_scale, False) for x in (before, after)]
    ks = [sides[0][0]] + [o[1] for o in own] + [sides[1][0]]
    vs = [sides[0][1]] + [o[2] for o in own] + [sides[1][1]]
    return attend(neighbours.reshape(-1), columns * size, [o[0] for o in own], ks, vs, fine_output, cu, lat, cells)


def solution(mesh):
    return jax.shard_map(
        shards,
        mesh=mesh,
        in_specs=(P("group", "lon", None, None), P(None, "lon", None), P("group"),
                  P(), P(), P(), P(), P(), P(), P(), P()),
        out_specs=P("group", "lon", None, None),
        check_vma=False,
    )
```

time: 124 us -> 163 us (1.31)
  Pallas kernels: 81.3 us -> 130 us
  local copies, waits for them, and re-layouts: 29.1 us -> 5.21 us
  waiting for transfers between devices: 0.02 us -> 15.5 us
    pallas_call x3 -> x5, Pallas kernels: 63 us -> 108 us  [the longest x1 64.6 us: edges(): pl.pallas_call(edges_kernel, in_specs=[ANY], out_specs=[ANY, ANY], out_sh...]
    ppermute x8, waiting for transfers between devices: 0.02 us -> 15.5 us  [the longest x6 15.5 us: gather_cells(): blocks.append(lax.ppermute(held, axis, pairs))]
    pad x8 -> x0, local copies, waits for them, and re-layouts: 12.5 us -> none  [the longest x4 6.9 us: shards(): pad_k = lambda a: jnp.pad(a, ((0, 0), (cells, cells), (0, 0)))]
    slice x7 -> x0, local copies, waits for them, and re-layouts: 8.38 us -> none  [the longest x1 3.14 us: shards(): q[c:c + 1]]
    pallas_call x3 -> x4, Pallas kernels: 18.2 us -> 22.1 us  [project(): pl.pallas_call(functools.partial(project_kernel, with_query, rows), grid=...]
    unnamed x38 -> x19, local copies, waits for them, and re-layouts: 5.21 us -> 4.41 us
  transfers between devices with their start and end apart: 8 -> 8, of which waited for: 0 -> 2; matrix products, arithmetic and copies ran while one was open for 17% -> 1% of each run, Pallas kernels for 17% -> 18%
where the time goes in v2:
time: 163 us
  Pallas kernels  130 us (80%)
  waiting for transfers between devices  15.5 us (10%)
  starting transfers between devices  11.7 us (7%)
  local copies, waits for them, and re-layouts  5.21 us (3%)
    pallas_call x1, Pallas kernels, edges(): pl.pallas_call(edges_kernel, in_specs=[ANY], out_specs=[ANY, ANY], out_sh...  64.6 us
    pallas_call x1, Pallas kernels, attend(): pl.pallas_call(functools.partial(attend_kernel, rows, ncol, total_columns...  30.1 us
    pallas_call x4, Pallas kernels, project(): pl.pallas_call(functools.partial(project_kernel, with_query, rows), grid=...  22.1 us
    ppermute x6, waiting for transfers between devices, gather_cells(): blocks.append(lax.ppermute(held, axis, pairs))  15.5 us
    pallas_call x1, Pallas kernels, coarse_level(): pl.pallas_call(functools.partial(coarse_kernel, len(blocks)), grid=(steps...  7.6 us
    ppermute x6, starting transfers between devices, gather_cells(): blocks.append(lax.ppermute(held, axis, pairs))  6.24 us
    ppermute x1, starting transfers between devices, shards(): after = lax.ppermute(first, 'lon', down)  5.5 us
    unnamed x19, local copies, waits for them, and re-layouts  4.41 us
  transfers between devices with their start and end apart: 8, of which 2 were waited for; matrix products, arithmetic and copies ran while one was open for 1% of the time, Pallas kernels for 18%

profile of v2, /device:TPU:0, one launch (start us, length us, event | category | flops | bytes accessed | tf_op | source)
XLA Modules:
  0.0 163.0 jit_solution(18390622690357342781)
XLA Ops:
  0.0 64.6 %edges.1 = (bf16[64,1,64,128]{3,2,1,0:T(8,128)(2,1)}, bf16[64,1,64,128]{3,2,1,0:T(8,128)(2,1)}) custom-call(bf16[64,2,64,128]{3,2,1,0:T(8,128)(2,1)} %tok_ref.7), custom_call_target="tpu_custom_call" | custom-call | tf_op jit(solution)/shard_map/edges/pallas_call | solution.py:73
  64.7 5.5 %collective-permute-start.1 = (bf16[64,1,64,128]{3,2,1,0:T(8,128)(2,1)}, bf16[64,1,64,128]{3,2,1,0:T(8,128)(2,1)S(1)}, u32[]{:S(2)}, u32[]{:S(2)}) collective-permute-start(bf16[64,1,64,128]{3,2,1,0:T(8,128)(2,1)} %get-tuple-element.26), channel_id=1, source_target_pairs={{1,0},{2,1},{3,2},{4,3},{5,4},{6,5},{7,6},{8,7},{9,8},{10,9},{11,1... | collective-permute-start | bytes 3145736 | tf_op jit(solution)/shard_map/ppermute | solution.py:390
  70.2 0.0 collective-permute-start
  70.8 4.1 %pool.1 = (f32[16,128]{1,0:T(8,128)}, f32[8,128]{1,0:T(8,128)}) custom-call(s32[1]{0:T(128)S(6)} %copy.17.step_ref, f32[8,128]{1,0:T(8,128)} %constant.8.clone.freq_ref, bf16[256,128]{1,0:T(8,128)(2,1)} %weight_ref.1, bf16[64,2,64,128]{3,2,1,0:T(8,128)(2,1)} %tok_ref.7), custom_call_target="tpu_custom_call" | custom-call | tf_op jit(solution)/shard_map/pool/pallas_call | solution.py:107
  74.9 0.0 collective-permute-start.4
  74.9 0.0 collective-permute-start.3
  74.9 1.9 %collective-permute-start.2 = (f32[16,128]{1,0:T(8,128)}, f32[16,128]{1,0:T(8,128)S(1)}, u32[]{:S(2)}, u32[]{:S(2)}) collective-permute-start(f32[16,128]{1,0:T(8,128)} %get-tuple-element.32.refs_0_), channel_id=1, source_target_pairs={{0,1},{1,0},{2,3},{3,2},{4,5},{5,4},{6,7},{7,6},{8,9},{9,8},{10,11... | collective-permute-start | bytes 24584 | tf_op jit(solution)/shard_map/ppermute | solution.py:142
  76.7 10.8 %collective-permute-done.4.refs_3_ = f32[16,128]{1,0:T(8,128)S(1)} collective-permute-done((f32[16,128]{1,0:T(8,128)}, f32[16,128]{1,0:T(8,128)S(1)}, u32[]{:S(2)}, u32[]{:S(2)}) %collective-permute-start.4) | collective-permute-done | bytes 8224 | tf_op jit(solution)/shard_map/ppermute | solution.py:142
  87.6 4.7 %collective-permute-done.3.refs_2_ = f32[16,128]{1,0:T(8,128)S(1)} collective-permute-done((f32[16,128]{1,0:T(8,128)}, f32[16,128]{1,0:T(8,128)S(1)}, u32[]{:S(2)}, u32[]{:S(2)}) %collective-permute-start.3) | collective-permute-done | bytes 8224 | tf_op jit(solution)/shard_map/ppermute | solution.py:142
  92.2 0.0 collective-permute-done.2.refs_1_
  92.3 0.6 copy-done.7
  92.8 0.6 copy-done.8
  93.4 1.4 join.1.refs_0_
  94.8 3.6 %collective-permute-start.7 = (f32[32,128]{1,0:T(8,128)}, f32[32,128]{1,0:T(8,128)S(1)}, u32[]{:S(2)}, u32[]{:S(2)}) collective-permute-start(f32[32,128]{1,0:T(8,128)} %join.1.refs_0_), channel_id=1, source_target_pairs={{0,12},{1,13},{2,14},{3,15},{4,8},{5,9},{6,10},{7,11},{8,4},{9,5},... | collective-permute-start | bytes 49160 | tf_op jit(solution)/shard_map/ppermute | solution.py:142
  98.4 0.8 collective-permute-start.5
  99.2 5.9 %project.5 = (bf16[4096,128]{1,0:T(8,128)(2,1)}, bf16[4224,128]{1,0:T(8,128)(2,1)}, bf16[33,128,128]{2,1,0:T(8,128)(2,1)}) custom-call(f32[2]{0:T(128)} %scale_ref.8, bf16[64,2,64,128]{3,2,1,0:T(8,128)(2,1)} %tok_ref.7, f32[8,128]{1,0:T(8,128)} %get-tuple-element.19.gain_ref, bf16[128,384]{1,0:T(8,128)(2,1)} %w_ref.7, bf16[256,128]{1,0:T(8,128)(2,1)} %constant.9.clone.ones_ref), custom_call_target="tpu_custom_call" | custom-call | tf_op jit(solution)/shard_map/project/pallas_call | solution.py:193
  105.1 5.9 %project.4 = (bf16[4096,128]{1,0:T(8,128)(2,1)}, bf16[4224,128]{1,0:T(8,128)(2,1)}, bf16[33,128,128]{2,1,0:T(8,128)(2,1)}) custom-call(f32[2]{0:T(128)} %scale_ref.8, bf16[64,2,64,128]{3,2,1,0:T(8,128)(2,1)} %tok_ref.7, f32[8,128]{1,0:T(8,128)} %get-tuple-element.19.gain_ref, bf16[128,384]{1,0:T(8,128)(2,1)} %w_ref.7, bf16[256,128]{1,0:T(8,128)(2,1)} %constant.9.clone.ones_ref), custom_call_target="tpu_custom_call" | custom-call | tf_op jit(solution)/shard_map/project/pallas_call | solution.py:193
  111.0 0.1 copy.16
  111.1 0.8 reshape.3.near_ref
  111.9 0.0 collective-permute-done.7.refs_3_
  111.9 0.0 collective-permute-done.6.refs_2_
  112.0 0.6 copy-done.2
  112.5 0.0 copy-done.3
  112.6 0.6 copy-done.4
  113.1 7.6 %coarse.1.refs_11_ = f32[16,128]{1,0:T(8,128)} custom-call(f32[16]{0:T(128)} %scale_ref.9, f32[32,128]{1,0:T(8,128)} %join.1.refs_0_, f32[32,128]{1,0:T(8,128)} %copy-done.4, f32[32,128]{1,0:T(8,128)} %copy-done.3, f32[32,128]{1,0:T(8,128)} %copy-done.2, bf16[128,1024]{1,0:T(8,128)(2,1)} %refs_4_.1, bf16[1024,3072]{1,0:T(8,128)(2,1)} %refs_7_.1, ...), custom_call_target="tpu_custom_call" | custom-call | tf_op jit(solution)/shard_map/coarse/pallas_call | solution.py:245
  120.8 0.0 copy-start.1
  120.8 1.0 copy-done.1
  121.7 5.1 %project.7 = (bf16[4224,128]{1,0:T(8,128)(2,1)}, bf16[33,128,128]{2,1,0:T(8,128)(2,1)}) custom-call(f32[2]{0:T(128)} %scale_ref.8, bf16[64,1,64,128]{3,2,1,0:T(8,128)(2,1)} %copy-done.1, f32[8,128]{1,0:T(8,128)} %get-tuple-element.19.gain_ref, bf16[128,384]{1,0:T(8,128)(2,1)} %w_ref.7, bf16[256,128]{1,0:T(8,128)(2,1)} %constant.9.clone.ones_ref), custom_call_target="tpu_custom_call" | custom-call | tf_op jit(solution)/shard_map/project/pallas_call | solution.py:193
  126.8 0.0 collective-permute-done.tok_ref
  126.8 1.0 copy-done
  127.8 5.1 %project.6 = (bf16[4224,128]{1,0:T(8,128)(2,1)}, bf16[33,128,128]{2,1,0:T(8,128)(2,1)}) custom-call(f32[2]{0:T(128)} %scale_ref.8, bf16[64,1,64,128]{3,2,1,0:T(8,128)(2,1)} %copy-done, f32[8,128]{1,0:T(8,128)} %get-tuple-element.19.gain_ref, bf16[128,384]{1,0:T(8,128)(2,1)} %w_ref.7, bf16[256,128]{1,0:T(8,128)(2,1)} %constant.9.clone.ones_ref), custom_call_target="tpu_custom_call" | custom-call | tf_op jit(solution)/shard_map/project/pallas_call | solution.py:193
  132.9 30.1 %attend.1 = bf16[64,2,64,128]{3,2,1,0:T(8,128)(2,1)} custom-call(s32[1152]{0:T(1024)} %reshape.3.near_ref, f32[4]{0:T(128)} %constant.11.clone.log_ref, bf16[4096,128]{1,0:T(8,128)(2,1)} %get-tuple-element.20.refs_0_, bf16[4096,128]{1,0:T(8,128)(2,1)} %get-tuple-element.21.refs_1_, bf16[4224,128]{1,0:T(8,128)(2,1)} %get-tuple-element.23.refs_2_, ...), custom_call_target="tpu_custom_call" | custom-call | tf_op jit(solution)/shard_map/attend/pallas_call | solution.py:368
  (13 shorter events, 0.0 us)
Async XLA Ops:
  64.7 56.1 %collective-permute-start.1 = (bf16[64,1,64,128]{3,2,1,0:T(8,128)(2,1)}, bf16[64,1,64,128]{3,2,1,0:T(8,128)(2,1)S(1)}, u32[]{:S(2)}, u32[]{:S(2)}) collective-permute-start(bf16[64,1,64,128]{3,2,1,0:T(8,128)(2,1)} %get-tuple-element.26), channel_id=1, source_target_pairs={{1,0},{2,1},{3,2},{4,3},{5,4},{6,5},{7,6},{8,7},{9,8},{10,9},{11,1... | collective-permute-start | bytes 3145736 | tf_op jit(solution)/shard_map/ppermute | solution.py:390
  70.2 56.7 %collective-permute-start = (bf16[64,1,64,128]{3,2,1,0:T(8,128)(2,1)}, bf16[64,1,64,128]{3,2,1,0:T(8,128)(2,1)S(1)}, u32[]{:S(2)}, u32[]{:S(2)}) collective-permute-start(bf16[64,1,64,128]{3,2,1,0:T(8,128)(2,1)} %get-tuple-element.22), channel_id=1, source_target_pairs={{0,1},{1,2},{2,3},{3,4},{4,5},{5,6},{6,7},{7,8},{8,9},{9,10},{10,1... | collective-permute-start | bytes 3145736 | tf_op jit(solution)/shard_map/ppermute | solution.py:389
  74.9 12.7 %collective-permute-start.4 = (f32[16,128]{1,0:T(8,128)}, f32[16,128]{1,0:T(8,128)S(1)}, u32[]{:S(2)}, u32[]{:S(2)}) collective-permute-start(f32[16,128]{1,0:T(8,128)} %get-tuple-element.32.refs_0_), channel_id=1, source_target_pairs={{0,3},{1,2},{2,1},{3,0},{4,7},{5,6},{6,5},{7,4},{8,11},{9,10},{10,... | collective-permute-start | bytes 24584 | tf_op jit(solution)/shard_map/ppermute | solution.py:142
  74.9 17.4 %collective-permute-start.3 = (f32[16,128]{1,0:T(8,128)}, f32[16,128]{1,0:T(8,128)S(1)}, u32[]{:S(2)}, u32[]{:S(2)}) collective-permute-start(f32[16,128]{1,0:T(8,128)} %get-tuple-element.32.refs_0_), channel_id=1, source_target_pairs={{0,2},{1,3},{2,0},{3,1},{4,6},{5,7},{6,4},{7,5},{8,10},{9,11},{10,... | collective-permute-start | bytes 24584 | tf_op jit(solution)/shard_map/ppermute | solution.py:142
  74.9 17.4 %collective-permute-start.2 = (f32[16,128]{1,0:T(8,128)}, f32[16,128]{1,0:T(8,128)S(1)}, u32[]{:S(2)}, u32[]{:S(2)}) collective-permute-start(f32[16,128]{1,0:T(8,128)} %get-tuple-element.32.refs_0_), channel_id=1, source_target_pairs={{0,1},{1,0},{2,3},{3,2},{4,5},{5,4},{6,7},{7,6},{8,9},{9,8},{10,11... | collective-permute-start | bytes 24584 | tf_op jit(solution)/shard_map/ppermute | solution.py:142
  87.6 4.7 %copy-start.6 = (f32[16,128]{1,0:T(8,128)}, f32[16,128]{1,0:T(8,128)S(1)}, u32[]{:S(2)}) copy-start(f32[16,128]{1,0:T(8,128)S(1)} %collective-permute-done.4.refs_3_) | copy-start | bytes 24580
  92.2 0.6 copy-start.7
  92.8 0.6 copy-start.8
  94.8 17.2 %collective-permute-start.7 = (f32[32,128]{1,0:T(8,128)}, f32[32,128]{1,0:T(8,128)S(1)}, u32[]{:S(2)}, u32[]{:S(2)}) collective-permute-start(f32[32,128]{1,0:T(8,128)} %join.1.refs_0_), channel_id=1, source_target_pairs={{0,12},{1,13},{2,14},{3,15},{4,8},{5,9},{6,10},{7,11},{8,4},{9,5},... | collective-permute-start | bytes 49160 | tf_op jit(solution)/shard_map/ppermute | solution.py:142
  98.4 13.6 %collective-permute-start.6 = (f32[32,128]{1,0:T(8,128)}, f32[32,128]{1,0:T(8,128)S(1)}, u32[]{:S(2)}, u32[]{:S(2)}) collective-permute-start(f32[32,128]{1,0:T(8,128)} %join.1.refs_0_), channel_id=1, source_target_pairs={{0,8},{1,9},{2,10},{3,11},{4,12},{5,13},{6,14},{7,15},{8,0},{9,1},... | collective-permute-start | bytes 49160 | tf_op jit(solution)/shard_map/ppermute | solution.py:142
  98.4 13.6 %collective-permute-start.5 = (f32[32,128]{1,0:T(8,128)}, f32[32,128]{1,0:T(8,128)S(1)}, u32[]{:S(2)}, u32[]{:S(2)}) collective-permute-start(f32[32,128]{1,0:T(8,128)} %join.1.refs_0_), channel_id=1, source_target_pairs={{0,4},{1,5},{2,6},{3,7},{4,0},{5,1},{6,2},{7,3},{8,12},{9,13},{10,... | collective-permute-start | bytes 49160 | tf_op jit(solution)/shard_map/ppermute | solution.py:142
  105.1 5.9 %copy-start.5 = (s32[64,2,9]{0,1,2:T(2,128)S(1)}, s32[64,2,9]{0,1,2:T(2,128)}, u32[]{:S(2)}) copy-start(s32[64,2,9]{0,1,2:T(2,128)} %param.16) | copy-start | bytes 13828
  111.9 0.6 copy-start.2
  112.0 0.6 copy-start.3
  112.6 0.6 copy-start.4
  120.8 1.0 copy-start.1
  126.8 1.0 copy-start
